TPU v7x, 512 devices: a whole 4x8x8 slice. The times are simulated.
512 devices in a mesh: row: 32 (over z, y_lo), col: 16 (over y_hi, x, core).
Axes of the slice: x: 4, y: 8 (y_hi: 2, y_lo: 4; y = y_hi * 4 + y_lo), z: 8, core: 2. Of those that a mesh axis runs over, the one named last changes fastest.
Arguments:
- features: bfloat16 [16, 4096, 128], P('col', 'row'), may hold values from -6 to 6
- weight1: bfloat16 [128, 128], replicated, may hold values from -0.5 to 0.5
- weight2: bfloat16 [128, 128], replicated, may hold values from -0.5 to 0.5
- tile_values: bfloat16 [32, 16, 96, 128, 128], P('row', 'col'), may hold values from -0.1875 to 0.1875
- tile_coords: int32 [32, 16, 2, 96], P('row', 'col'), may hold values from 0 to 31, as said below
- tile_count: int32 [32, 16], P('row', 'col'), may hold values from 1 to 96, as said below
- out_grad: bfloat16 [16, 4096, 128], P('col', 'row'), may hold values from -6 to 6
Outputs:
- output: bfloat16 [16, 4096, 128], P('col', 'row')
- grad_features: bfloat16 [16, 4096, 128], P('col', 'row')
- grad_weight1: float32 [128, 128], replicated
- grad_weight2: float32 [128, 128], replicated
Inputs may be any that keep to these rules, and one draw needn't show every extreme that they name: On each device tile_coords[r, c, 0, t] is below 16 and tile_coords[r, c, 1, t] below 32; no block position appears twice among a device's 96 slots. `tile_count`: some device has all 96 slots live.
All inputs are finite; a program needn't handle non-finite values.
Results may differ from a plain program's by a relative error of at most 0.034.
Values may be sent and summed in bfloat16 or wider, within the bound.
No kernel may reach another device: no remote copies, remote signals or barrier semaphores. Data moves between devices by JAX's collectives and lax.ppermute only.
A program may use at most 64 MiB of HBM per device.

v0:
```python
import math
import jax
import jax.numpy as jnp
from jax import lax
from jax.sharding import PartitionSpec as P


def forward_part(local_tiles, row_ids, col_ids, live_slots, panel_rows, row_blocks):
    block_side = local_tiles.shape[1]
    feat_width = panel_rows.shape[-1]
    blocks = panel_rows.reshape(-1, block_side, feat_width)[col_ids]
    products = jnp.einsum("tij,tjf->tif", local_tiles, blocks, preferred_element_type=jnp.float32)
    onehot = jnp.where(
        (row_ids[None, :] == jnp.arange(row_blocks, dtype=jnp.int32)[:, None])
        & live_slots[None, :],
        1.0,
        0.0,
    ).astype(jnp.float32)
    return jnp.einsum("rt,tif->rif", onehot, products).reshape(row_blocks * block_side, feat_width)


def transposed_part(local_tiles, row_ids, col_ids, live_slots, panel_rows, col_blocks):
    block_side = local_tiles.shape[1]
    feat_width = panel_rows.shape[-1]
    blocks = panel_rows.reshape(-1, block_side, feat_width)[row_ids]
    products = jnp.einsum("tji,tjf->tif", local_tiles, blocks, preferred_element_type=jnp.float32)
    onehot = jnp.where(
        (col_ids[None, :] == jnp.arange(col_blocks, dtype=jnp.int32)[:, None])
        & live_slots[None, :],
        1.0,
        0.0,
    ).astype(jnp.float32)
    return jnp.einsum("ct,tif->cif", onehot, products).reshape(col_blocks * block_side, feat_width)


def silu_slope(value):
    sigmoid = jax.nn.sigmoid(value)
    return sigmoid * (1.0 + value * (1.0 - sigmoid))


def on_device(features, weight1, weight2, tile_values, tile_coords, tile_count, out_grad):
    local_tiles = tile_values[0, 0]
    row_ids = tile_coords[0, 0, 0]
    col_ids = tile_coords[0, 0, 1]
    slot_total = local_tiles.shape[0]
    live_slots = jnp.arange(slot_total, dtype=jnp.int32) < tile_count[0, 0]
    block_side = local_tiles.shape[1]
    shard_rows = features.shape[1]
    row_blocks = shard_rows * lax.axis_size("col") // block_side
    col_blocks = shard_rows * lax.axis_size("row") // block_side
    node_total = shard_rows * lax.axis_size("row") * lax.axis_size("col")
    grad_local = out_grad[0]
    grad_two = jnp.dot(grad_local, weight2.T, preferred_element_type=jnp.float32).astype(
        jnp.bfloat16
    )
    gathered = lax.all_gather(features, "row", axis=1, tiled=True)[0]
    grad_rows = lax.all_gather(grad_two, "row", axis=0, tiled=True)
    part_one = forward_part(local_tiles, row_ids, col_ids, live_slots, gathered, row_blocks)
    part_three = forward_part(local_tiles, row_ids, col_ids, live_slots, grad_rows, row_blocks)
    agg_sum, grad_hidden = (
        lax.psum_scatter(
            part_one.astype(jnp.bfloat16), "col", scatter_dimension=0, tiled=True
        ).astype(jnp.float32),
        lax.psum_scatter(
            part_three.astype(jnp.bfloat16), "col", scatter_dimension=0, tiled=True
        ).astype(jnp.float32),
    )
    agg_one = agg_sum.astype(jnp.bfloat16)
    pre_one = jnp.dot(agg_one, weight1, preferred_element_type=jnp.float32)
    hidden = jax.nn.silu(pre_one).astype(jnp.bfloat16)
    hidden_rows = lax.all_gather(hidden, "col", axis=0, tiled=True)
    part_two = transposed_part(local_tiles, row_ids, col_ids, live_slots, hidden_rows, col_blocks)
    agg_two = lax.psum_scatter(
        part_two.astype(jnp.bfloat16), "row", scatter_dimension=0, tiled=True
    )
    output = jnp.dot(agg_two, weight2, preferred_element_type=jnp.float32).astype(jnp.bfloat16)
    grad_pre = (grad_hidden * silu_slope(pre_one)).astype(jnp.bfloat16)
    grad_one = jnp.dot(grad_pre, weight1.T, preferred_element_type=jnp.float32).astype(jnp.bfloat16)
    grad_hidden_rows = lax.all_gather(grad_one, "col", axis=0, tiled=True)
    part_four = transposed_part(
        local_tiles, row_ids, col_ids, live_slots, grad_hidden_rows, col_blocks
    )
    grad_features = lax.psum_scatter(
        part_four.astype(jnp.bfloat16), "row", scatter_dimension=0, tiled=True
    )
    contract = (((0,), (0,)), ((), ()))
    weight_one = lax.dot_general(agg_one, grad_pre, contract, preferred_element_type=jnp.float32)
    weight_two = lax.dot_general(agg_two, grad_local, contract, preferred_element_type=jnp.float32)
    sum_one, sum_two = lax.psum((weight_one, weight_two), ("row", "col"))
    factor = 1.0 / math.sqrt(node_total)
    return (output[None], grad_features[None], sum_one * factor, sum_two * factor)


def solution(mesh):
    placed = (
        P("col", "row", None),
        P(),
        P(),
        P("row", "col", None, None, None),
        P("row", "col", None, None),
        P("row", "col"),
        P("col", "row", None),
    )
    return jax.shard_map(
        on_device,
        mesh=mesh,
        in_specs=placed,
        out_specs=(P("col", "row", None), P("col", "row", None), P(), P()),
        check_vma=False,
    )
```

profile of v0, /device:TPU:2, one launch (start us, length us, event | category | flops | bytes accessed | tf_op | source)
XLA Modules:
  0.0 1141.4 jit_solution(11435500891429155768)
XLA Ops:
  11.9 156.6 %all-gather.5.cloned.1.call-done = bf16[4096,128]{1,0:T(8,128)(2,1)} async-done(((bf16[128,128]{1,0:T(8,128)(2,1)}), bf16[4096,128]{1,0:T(8,128)(2,1)}) %all-gather.5.cloned.1.call-update) | async-done | bytes 1048592 | tf_op jit(solution)/shard_map/all_gather | solution.py:57
  168.5 3.9 gather_fusion.2
  172.5 5.9 fusion.10
  178.4 5.0 copy.18
  183.3 2.4 fusion.25
  186.8 137.2 %all-gather.3.cloned.1.call-done = bf16[1,4096,128]{2,1,0:T(8,128)(2,1)} async-done(((bf16[1,128,128]{2,1,0:T(8,128)(2,1)}), bf16[1,4096,128]{2,1,0:T(8,128)(2,1)}) %all-gather.3.cloned.1.call-update) | async-done | bytes 1048592 | tf_op jit(solution)/shard_map/all_gather | solution.py:56
  324.0 3.9 gather_fusion
  327.9 5.9 fusion.14
  333.9 5.0 copy.16
  342.3 71.1 %reduce-scatter.9.cloned.1.call-done = bf16[128,128]{1,0:T(8,128)(2,1)} async-done(((bf16[2048,128]{1,0:T(8,128)(2,1)}), bf16[128,128]{1,0:T(8,128)(2,1)}) %reduce-scatter.9.cloned.1.call-update) | async-done | bytes 32784 | tf_op jit(solution)/shard_map/reduce_scatter | solution.py:64
  413.4 86.4 %reduce-scatter.5.cloned.1.call-done = bf16[128,128]{1,0:T(8,128)(2,1)} async-done(((bf16[2048,128]{1,0:T(8,128)(2,1)}), bf16[128,128]{1,0:T(8,128)(2,1)}) %reduce-scatter.5.cloned.1.call-update) | async-done | bytes 32784 | tf_op jit(solution)/shard_map/reduce_scatter | solution.py:61
  500.8 27.9 %all_gather.13 = bf16[2048,128]{1,0:T(8,128)(2,1)} all-gather(bf16[128,128]{1,0:T(8,128)(2,1)S(1)} %get-tuple-element.7), channel_id=1, replica_groups=mesh['row'=32,'col'=16] {'col'}, dimensions={0}, use_global_device_ids=true | all-gather | bytes 557056 | tf_op jit(solution)/shard_map/all_gather | solution.py:71
  528.7 3.7 gather_fusion.1
  532.4 4.8 fusion.12
  537.2 5.0 copy.17
  542.2 2.4 fusion.16
  546.2 29.6 %all_gather.15 = bf16[2048,128]{1,0:T(8,128)(2,1)} all-gather(bf16[128,128]{1,0:T(8,128)(2,1)S(1)} %convolution_convert_fusion), channel_id=1, replica_groups=mesh['row'=32,'col'=16] {'col'}, dimensions={0}, use_global_device_ids=true | all-gather | bytes 557056 | tf_op jit(solution)/shard_map/all_gather | solution.py:79
  575.8 3.7 gather_fusion.3
  579.6 4.8 fusion.8
  584.4 5.0 copy.19
  590.2 120.2 %reduce-scatter.7.cloned.1.call-done = bf16[128,128]{1,0:T(8,128)(2,1)} async-done(((bf16[4096,128]{1,0:T(8,128)(2,1)}), bf16[128,128]{1,0:T(8,128)(2,1)}) %reduce-scatter.7.cloned.1.call-update) | async-done | bytes 32784 | tf_op jit(solution)/shard_map/reduce_scatter | solution.py:73
  712.0 2.4 fusion.19
  716.7 255.6 %all-reduce.3.cloned.1.call-done = (f32[128,128]{1,0:T(8,128)}, f32[128,128]{1,0:T(8,128)}) async-done(((f32[128,128]{1,0:T(8,128)}, f32[128,128]{1,0:T(8,128)}), (f32[128,128]{1,0:T(8,128)}, f32[128,128]{1,0:T(8,128)})) %all-reduce.3.cloned.1.call-update) | async-done | bytes 131088 | tf_op jit(solution)/shard_map/psum | solution.py:89
  973.8 160.8 %reduce-scatter.11.cloned.1.call-done = bf16[128,128]{1,0:T(8,128)(2,1)} async-done(((bf16[4096,128]{1,0:T(8,128)(2,1)}), bf16[128,128]{1,0:T(8,128)(2,1)}) %reduce-scatter.11.cloned.1.call-update) | async-done | bytes 32784 | tf_op jit(solution)/shard_map/reduce_scatter | solution.py:83
  (43 shorter events, 17.2 us)
Async XLA Ops:
  7.2 165.3 %copy-start = (bf16[1,1,96,128,128]{4,3,2,1,0:T(8,128)(2,1)S(1)}, bf16[1,1,96,128,128]{4,3,2,1,0:T(8,128)(2,1)}, u32[]{:S(2)}) copy-start(bf16[1,1,96,128,128]{4,3,2,1,0:T(8,128)(2,1)} %param.10) | copy-start | bytes 9437188
  7.2 161.4 %all-gather.5.cloned.1.call-start = ((), (), s32[]{:S(2)}) async-start(), calls=%async_computation.7 | async-start | bytes 1081344 | tf_op jit(solution)/shard_map/all_gather | solution.py:57
  8.9 315.1 %all-gather.3.cloned.1.call-start = ((), (), s32[]{:S(2)}) async-start(), calls=%async_computation.4 | async-start | bytes 1081344 | tf_op jit(solution)/shard_map/all_gather | solution.py:56
  9.7 403.7 %reduce-scatter.9.cloned.1.call-start = ((), (), s32[]{:S(2)}) async-start(), calls=%async_computation.8 | async-start | bytes 557056 | tf_op jit(solution)/shard_map/reduce_scatter | solution.py:64
  186.7 313.1 %reduce-scatter.5.cloned.1.call-start = ((), (), s32[]{:S(2)}) async-start(), calls=%async_computation.5 | async-start | bytes 557056 | tf_op jit(solution)/shard_map/reduce_scatter | solution.py:61
  338.8 161.0 %copy-start.4 = (bf16[128,128]{1,0:T(8,128)(2,1)S(1)}, bf16[128,128]{1,0:T(8,128)(2,1)}, u32[]{:S(2)}) copy-start(bf16[128,128]{1,0:T(8,128)(2,1)} %param.8) | copy-start | bytes 98308
  342.2 368.2 %reduce-scatter.7.cloned.1.call-start = ((), (), s32[]{:S(2)}) async-start(), calls=%async_computation.6 | async-start | bytes 1081344 | tf_op jit(solution)/shard_map/reduce_scatter | solution.py:73
  546.0 426.2 %all-reduce.3.cloned.1.call-start = ((), (), s32[]{:S(2)}) async-start(), calls=%async_computation.10 | async-start | bytes 262144 | tf_op jit(solution)/shard_map/psum | solution.py:89
  584.4 5.0 copy-start.5
  584.4 126.0 %copy-start.2 = (bf16[1,128,128]{2,1,0:T(8,128)(2,1)S(1)}, bf16[1,128,128]{2,1,0:T(8,128)(2,1)}, u32[]{:S(2)}) copy-start(bf16[1,128,128]{2,1,0:T(8,128)(2,1)} %param.13) | copy-start | bytes 98308
  712.0 3.9 copy-start.1
  712.0 3.9 copy-start.3
  712.0 422.6 %reduce-scatter.11.cloned.1.call-start = ((), (), s32[]{:S(2)}) async-start(), calls=%async_computation.9 | async-start | bytes 1081344 | tf_op jit(solution)/shard_map/reduce_scatter | solution.py:83
Sparse Core Ops, SparseCore 0:
  10.7 157.8 all-gather.4
  170.6 153.3 all-gather.2
  328.7 84.6 reduce-scatter.8
  418.5 81.2 reduce-scatter.4
  546.1 164.1 reduce-scatter.6
  716.9 255.3 all-reduce.2
  975.6 158.9 reduce-scatter.10
where the time goes:
time: 1140 us
  waiting for transfers between devices  989 us (87%)
  blocking collectives  57.6 us (5%)
  local copies, waits for them, and re-layouts  40.6 us (4%)
  matrix products  37 us (3%)
  between operations  14.9 us (1%)
    psum x1, waiting for transfers between devices, on_device(): sum_one, sum_two = lax.psum((weight_one, weight_two), ('row', 'col'))  256 us
    reduce_scatter x1, waiting for transfers between devices, on_device(): lax.psum_scatter(part_four.astype(jnp.bfloat16), 'row', scatter_dimension...  161 us
    all_gather x1, waiting for transfers between devices, on_device(): grad_rows = lax.all_gather(grad_two, 'row', axis=0, tiled=True)  157 us
    all_gather x1, waiting for transfers between devices, on_device(): gathered = lax.all_gather(features, 'row', axis=1, tiled=True)[0]  137 us
    reduce_scatter x1, waiting for transfers between devices, on_device(): lax.psum_scatter(part_two.astype(jnp.bfloat16), 'row', scatter_dimension=...  120 us
    reduce_scatter x1, waiting for transfers between devices, on_device(): lax.psum_scatter(part_one.astype(jnp.bfloat16), 'col', scatter_dimension=...  86.4 us
    reduce_scatter x1, waiting for transfers between devices, on_device(): lax.psum_scatter(part_three.astype(jnp.bfloat16), 'col', scatter_dimensio...  71.1 us
    all_gather x1, blocking collectives, on_device(): grad_hidden_rows = lax.all_gather(grad_one, 'col', axis=0, tiled=True)  29.6 us
  transfers between devices with their start and end apart: 7, of which 7 were waited for; matrix products, arithmetic and copies ran while one was open for 5% of the time, Pallas kernels for 0%

commit v1 on v0

--- a/solution.py
+++ b/solution.py
@@ -86,7 +86,7 @@
     contract = (((0,), (0,)), ((), ()))
     weight_one = lax.dot_general(agg_one, grad_pre, contract, preferred_element_type=jnp.float32)
     weight_two = lax.dot_general(agg_two, grad_local, contract, preferred_element_type=jnp.float32)
-    sum_one, sum_two = lax.psum((weight_one, weight_two), ("row", "col"))
+    sum_one, sum_two = lax.psum(lax.psum((weight_one, weight_two), "row"), "col")
     factor = 1.0 / math.sqrt(node_total)
     return (output[None], grad_features[None], sum_one * factor, sum_two * factor)
 

time: 1140 us -> 1350 us (1.18)
  the two profiles are of different devices: /device:TPU:2 before, /device:TPU:6 now
where the time goes in v1:
time: 1350 us
  waiting for transfers between devices  1200 us (89%)
  blocking collectives  55.9 us (4%)
  local copies, waits for them, and re-layouts  40.5 us (3%)
  matrix products  37 us (3%)
  between operations  14.9 us (1%)
    psum x1, waiting for transfers between devices, on_device(): lax.psum((weight_one, weight_two), 'row')  270 us
    psum x1, waiting for transfers between devices, on_device(): lax.psum(lax.psum((weight_one, weight_two), 'row'), 'col')  174 us
    reduce_scatter x1, waiting for transfers between devices, on_device(): lax.psum_scatter(part_four.astype(jnp.bfloat16), 'row', scatter_dimension...  169 us
    all_gather x1, waiting for transfers between devices, on_device(): grad_rows = lax.all_gather(grad_two, 'row', axis=0, tiled=True)  157 us
    all_gather x1, waiting for transfers between devices, on_device(): gathered = lax.all_gather(features, 'row', axis=1, tiled=True)[0]  137 us
    reduce_scatter x1, waiting for transfers between devices, on_device(): lax.psum_scatter(part_two.astype(jnp.bfloat16), 'row', scatter_dimension=...  132 us
    reduce_scatter x1, waiting for transfers between devices, on_device(): lax.psum_scatter(part_one.astype(jnp.bfloat16), 'col', scatter_dimension=...  86.5 us
    reduce_scatter x1, waiting for transfers between devices, on_device(): lax.psum_scatter(part_three.astype(jnp.bfloat16), 'col', scatter_dimensio...  70.8 us
  transfers between devices with their start and end apart: 8, of which 8 were waited for; matrix products, arithmetic and copies ran while one was open for 4% of the time, Pallas kernels for 0%

profile of v1, /device:TPU:6, one launch (start us, length us, event | category | flops | bytes accessed | tf_op | source)
XLA Modules:
  0.0 1347.9 jit_solution(10883201379877712381)
XLA Ops:
  11.9 156.7 %all-gather.5.cloned.1.call-done = bf16[4096,128]{1,0:T(8,128)(2,1)} async-done(((bf16[128,128]{1,0:T(8,128)(2,1)}), bf16[4096,128]{1,0:T(8,128)(2,1)}) %all-gather.5.cloned.1.call-update) | async-done | bytes 1048592 | tf_op jit(solution)/shard_map/all_gather | solution.py:57
  168.6 3.9 gather_fusion.2
  172.5 5.9 fusion.10
  178.5 4.9 copy.18
  186.8 137.4 %all-gather.3.cloned.1.call-done = bf16[1,4096,128]{2,1,0:T(8,128)(2,1)} async-done(((bf16[1,128,128]{2,1,0:T(8,128)(2,1)}), bf16[1,4096,128]{2,1,0:T(8,128)(2,1)}) %all-gather.3.cloned.1.call-update) | async-done | bytes 1048592 | tf_op jit(solution)/shard_map/all_gather | solution.py:56
  324.2 3.9 gather_fusion
  328.2 5.9 fusion.14
  334.1 4.9 copy.16
  342.4 70.8 %reduce-scatter.9.cloned.1.call-done = bf16[128,128]{1,0:T(8,128)(2,1)} async-done(((bf16[2048,128]{1,0:T(8,128)(2,1)}), bf16[128,128]{1,0:T(8,128)(2,1)}) %reduce-scatter.9.cloned.1.call-update) | async-done | bytes 32784 | tf_op jit(solution)/shard_map/reduce_scatter | solution.py:64
  413.3 86.5 %reduce-scatter.5.cloned.1.call-done = bf16[128,128]{1,0:T(8,128)(2,1)} async-done(((bf16[2048,128]{1,0:T(8,128)(2,1)}), bf16[128,128]{1,0:T(8,128)(2,1)}) %reduce-scatter.5.cloned.1.call-update) | async-done | bytes 32784 | tf_op jit(solution)/shard_map/reduce_scatter | solution.py:61
  500.7 26.3 %all_gather.13 = bf16[2048,128]{1,0:T(8,128)(2,1)} all-gather(bf16[128,128]{1,0:T(8,128)(2,1)S(1)} %get-tuple-element.9), channel_id=1, replica_groups=mesh['row'=32,'col'=16] {'col'}, dimensions={0}, use_global_device_ids=true | all-gather | bytes 557056 | tf_op jit(solution)/shard_map/all_gather | solution.py:71
  527.0 3.7 gather_fusion.1
  530.8 4.8 fusion.12
  535.5 4.9 copy.17
  540.5 2.4 fusion.16
  544.5 29.6 %all_gather.15 = bf16[2048,128]{1,0:T(8,128)(2,1)} all-gather(bf16[128,128]{1,0:T(8,128)(2,1)S(1)} %convolution_convert_fusion), channel_id=1, replica_groups=mesh['row'=32,'col'=16] {'col'}, dimensions={0}, use_global_device_ids=true | all-gather | bytes 557056 | tf_op jit(solution)/shard_map/all_gather | solution.py:79
  574.1 3.8 gather_fusion.3
  578.6 131.6 %reduce-scatter.7.cloned.1.call-done = bf16[128,128]{1,0:T(8,128)(2,1)} async-done(((bf16[4096,128]{1,0:T(8,128)(2,1)}), bf16[128,128]{1,0:T(8,128)(2,1)}) %reduce-scatter.7.cloned.1.call-update) | async-done | bytes 32784 | tf_op jit(solution)/shard_map/reduce_scatter | solution.py:73
  712.1 4.8 fusion.8
  716.9 4.9 copy.19
  721.8 270.4 %all-reduce.5.cloned.1.call-done = (f32[128,128]{1,0:T(8,128)}, f32[128,128]{1,0:T(8,128)}) async-done(((f32[128,128]{1,0:T(8,128)}, f32[128,128]{1,0:T(8,128)}), (f32[128,128]{1,0:T(8,128)}, f32[128,128]{1,0:T(8,128)})) %all-reduce.5.cloned.1.call-update) | async-done | bytes 131088 | tf_op jit(solution)/shard_map/psum | solution.py:89
  992.4 2.4 fusion.19
  997.0 173.5 %all-reduce.7.cloned.1.call-done = (f32[128,128]{1,0:T(8,128)}, f32[128,128]{1,0:T(8,128)}) async-done(((f32[128,128]{1,0:T(8,128)}, f32[128,128]{1,0:T(8,128)}), (f32[128,128]{1,0:T(8,128)}, f32[128,128]{1,0:T(8,128)})) %all-reduce.7.cloned.1.call-update) | async-done | bytes 131088 | tf_op jit(solution)/shard_map/psum | solution.py:89
  1172.1 169.0 %reduce-scatter.11.cloned.1.call-done = bf16[128,128]{1,0:T(8,128)(2,1)} async-done(((bf16[4096,128]{1,0:T(8,128)(2,1)}), bf16[128,128]{1,0:T(8,128)(2,1)}) %reduce-scatter.11.cloned.1.call-update) | async-done | bytes 32784 | tf_op jit(solution)/shard_map/reduce_scatter | solution.py:83
  (46 shorter events, 19.9 us)
Async XLA Ops:
  7.2 165.4 %copy-start = (bf16[1,1,96,128,128]{4,3,2,1,0:T(8,128)(2,1)S(1)}, bf16[1,1,96,128,128]{4,3,2,1,0:T(8,128)(2,1)}, u32[]{:S(2)}) copy-start(bf16[1,1,96,128,128]{4,3,2,1,0:T(8,128)(2,1)} %param.10) | copy-start | bytes 9437188
  7.2 161.4 %all-gather.5.cloned.1.call-start = ((), (), s32[]{:S(2)}) async-start(), calls=%async_computation.7 | async-start | bytes 1081344 | tf_op jit(solution)/shard_map/all_gather | solution.py:57
  8.9 315.3 %all-gather.3.cloned.1.call-start = ((), (), s32[]{:S(2)}) async-start(), calls=%async_computation.4 | async-start | bytes 1081344 | tf_op jit(solution)/shard_map/all_gather | solution.py:56
  9.7 403.6 %reduce-scatter.9.cloned.1.call-start = ((), (), s32[]{:S(2)}) async-start(), calls=%async_computation.8 | async-start | bytes 557056 | tf_op jit(solution)/shard_map/reduce_scatter | solution.py:64
  186.8 312.9 %reduce-scatter.5.cloned.1.call-start = ((), (), s32[]{:S(2)}) async-start(), calls=%async_computation.5 | async-start | bytes 557056 | tf_op jit(solution)/shard_map/reduce_scatter | solution.py:61
  339.0 160.7 %copy-start.4 = (bf16[128,128]{1,0:T(8,128)(2,1)S(1)}, bf16[128,128]{1,0:T(8,128)(2,1)}, u32[]{:S(2)}) copy-start(bf16[128,128]{1,0:T(8,128)(2,1)} %param.8) | copy-start | bytes 98308
  342.4 367.9 %reduce-scatter.7.cloned.1.call-start = ((), (), s32[]{:S(2)}) async-start(), calls=%async_computation.6 | async-start | bytes 1081344 | tf_op jit(solution)/shard_map/reduce_scatter | solution.py:73
  544.3 447.9 %all-reduce.5.cloned.1.call-start = ((), (), s32[]{:S(2)}) async-start(), calls=%async_computation.10 | async-start | bytes 262144 | tf_op jit(solution)/shard_map/psum | solution.py:89
  574.1 3.8 copy-start.5
  574.1 136.2 %copy-start.2 = (bf16[1,128,128]{2,1,0:T(8,128)(2,1)S(1)}, bf16[1,128,128]{2,1,0:T(8,128)(2,1)}, u32[]{:S(2)}) copy-start(bf16[1,128,128]{2,1,0:T(8,128)(2,1)} %param.13) | copy-start | bytes 98308
  711.9 458.6 %all-reduce.7.cloned.1.call-start = ((), (), s32[]{:S(2)}) async-start(), calls=%async_computation.11 | async-start | bytes 262144 | tf_op jit(solution)/shard_map/psum | solution.py:89
  992.3 3.9 copy-start.1
  992.3 3.9 copy-start.3
  992.3 348.7 %reduce-scatter.11.cloned.1.call-start = ((), (), s32[]{:S(2)}) async-start(), calls=%async_computation.9 | async-start | bytes 1081344 | tf_op jit(solution)/shard_map/reduce_scatter | solution.py:83
Sparse Core Ops, SparseCore 0:
  10.7 157.8 all-gather.4
  170.7 153.4 all-gather.2
  328.9 84.3 reduce-scatter.8
  418.4 81.2 reduce-scatter.4
  544.5 165.7 reduce-scatter.6
  714.0 278.2 all-reduce.4
  995.2 175.2 all-reduce.6
  1174.1 166.8 reduce-scatter.10
